TPU v7x, 256 devices: a whole 4x4x8 slice. The times are simulated.
256 devices in a mesh: blk: 64 (over z, y, x_lo), feat: 4 (over x_hi, core).
Axes of the slice: x: 4 (x_hi: 2, x_lo: 2; x = x_hi * 2 + x_lo), y: 4, z: 8, core: 2. Of those that a mesh axis runs over, the one named last changes fastest.
Arguments:
- x_t: bfloat16 [256, 262144], P('feat', 'blk'), may hold values from -6 to 6
- weight: bfloat16 [256, 256], P('feat'), may hold values from -0.375 to 0.375
- cotangent: bfloat16 [256, 262144], P('feat', 'blk'), may hold values from -6 to 6
- tile_row: int32 [18432], P('blk'), may hold values from 0 to 31
- tile_col: int32 [18432], P('blk'), may hold values from 0 to 31
- tile_off: int32 [18432], P('blk'), may hold values from -4 to 4, as said below
- tile_vals: bfloat16 [18432, 128, 128], P('blk'), may hold values from -0.625 to 0.625
- tile_count: int32 [64], P('blk'), may hold values from 72 to 288, as said below
Outputs:
- out_t: bfloat16 [256, 262144], P('feat', 'blk')
- grad_x_t: bfloat16 [256, 262144], P('feat', 'blk')
- grad_weight: float32 [256, 256], P('feat')
Inputs may be any that keep to these rules, and one draw needn't show every extreme that they name: `tile_off`: slots 0 to 8 of every partition name each offset once; slots may repeat a tile position, and repeated tiles add. `tile_count`: some partition lists 288 live tiles and some 288 // 4.
All inputs are finite; a program needn't handle non-finite values.
Results may differ from a plain program's by a relative error of at most 0.0062.
Values may be sent and summed in bfloat16 or wider, within the bound.
No kernel may reach another device: no remote copies, remote signals or barrier semaphores. Data moves between devices by JAX's collectives and lax.ppermute only.
A program may use at most 128 MiB of HBM per device.

v0:
```python
import math
import jax
import jax.numpy as jnp
from jax import lax
from jax.sharding import PartitionSpec as P

REACH = 4


def shifted(block, axis, distance):
    devices = range(lax.axis_size(axis))
    route = [((i - distance) % len(devices), i) for i in devices]
    return lax.ppermute(block, axis, route)


def silu_slope(value):
    sig = jax.nn.sigmoid(value)
    return sig * (1.0 + value * (1.0 - sig))


def per_device(x_t, weight, cotangent, tile_row, tile_col, tile_off, tile_vals, tile_count):
    feat_rows = x_t.shape[0]
    nodes = x_t.shape[1]
    tile = tile_vals.shape[1]
    tiles = nodes // tile
    slots = tile_row.shape[0]
    span = 2 * REACH + 1
    w_cols = weight
    proj = lax.psum_scatter(
        lax.dot_general(w_cols, x_t, (((0,), (0,)), ((), ())), preferred_element_type=jnp.float32),
        "feat",
        scatter_dimension=0,
        tiled=True,
    ).astype(jnp.bfloat16)
    slab = proj.reshape(feat_rows, tiles, tile)
    fetched = {0: slab}
    for offset in range(-REACH, REACH + 1):
        if offset != 0:
            fetched[offset] = shifted(slab, "blk", -offset)
    stacked = jnp.concatenate([fetched[offset] for offset in range(-REACH, REACH + 1)], axis=1)
    live = (jnp.arange(slots, dtype=jnp.int32) < tile_count[0]).astype(jnp.float32)
    source_index = (tile_off + REACH) * tiles + tile_col
    pieces = jnp.take(stacked, source_index, axis=1)
    product = jnp.einsum("hsk,srk->hsr", pieces, tile_vals, preferred_element_type=jnp.float32)
    row_hot = (tile_row[:, None] == jnp.arange(tiles, dtype=jnp.int32)[None, :]).astype(
        jnp.float32
    ) * live[:, None]
    summed = jnp.einsum("hsr,st->htr", product, row_hot, precision=lax.Precision.HIGHEST)
    pre_t = summed.reshape(feat_rows, nodes)
    out_t = jax.nn.silu(pre_t).astype(jnp.bfloat16)
    grad_pre = (cotangent.astype(jnp.float32) * silu_slope(pre_t)).astype(jnp.bfloat16)
    grad_pieces = jnp.take(grad_pre.reshape(feat_rows, tiles, tile), tile_row, axis=1)
    contrib = jnp.einsum("hsr,srk->hsk", grad_pieces, tile_vals, preferred_element_type=jnp.float32)
    dest_hot = (source_index[:, None] == jnp.arange(span * tiles, dtype=jnp.int32)[None, :]).astype(
        jnp.float32
    ) * live[:, None]
    buffers = jnp.einsum("hsk,sd->hdk", contrib, dest_hot, precision=lax.Precision.HIGHEST)

    def bound_for(offset):
        return buffers[:, (offset + REACH) * tiles : (offset + REACH + 1) * tiles, :]

    gathered_sum = bound_for(0)
    for offset in range(-REACH, REACH + 1):
        if offset != 0:
            gathered_sum = gathered_sum + shifted(bound_for(offset), "blk", offset)
    grad_proj = gathered_sum.reshape(feat_rows, nodes).astype(jnp.bfloat16)
    piece = lax.all_gather(grad_proj, "feat", axis=0, tiled=True)
    block = lax.dot_general(
        x_t, piece, (((1,), (1,)), ((), ())), preferred_element_type=jnp.float32
    )
    weight_grad = block
    w_cols = weight
    input_grad = jnp.dot(w_cols, piece, preferred_element_type=jnp.float32)
    weight_grad, input_grad = (weight_grad, input_grad)
    factor = 1.0 / math.sqrt(nodes * lax.axis_size("blk"))
    weight_grad = lax.psum(weight_grad * factor, "blk")
    return (out_t, input_grad.astype(jnp.bfloat16), weight_grad)


def solution(mesh):
    placed = (
        P("feat", "blk"),
        P("feat", None),
        P("feat", "blk"),
        P("blk"),
        P("blk"),
        P("blk"),
        P("blk", None, None),
        P("blk"),
    )
    return jax.shard_map(
        per_device,
        mesh=mesh,
        in_specs=placed,
        out_specs=(P("feat", "blk"), P("feat", "blk"), P("feat", None)),
        check_vma=False,
    )
```

profile of v0, /device:TPU:26, one launch (start us, length us, event | category | flops | bytes accessed | tf_op | source)
XLA Modules:
  0.0 1056.2 jit_solution(13803362977749975269)
XLA Ops:
  8.2 3.4 fusion.58
  11.8 58.4 %reduce-scatter.2.cloned.1.call-done = f32[64,4096]{1,0:T(8,128)} async-done(((f32[256,4096]{1,0:T(8,128)}), f32[64,4096]{1,0:T(8,128)}) %reduce-scatter.2.cloned.1.call-update) | async-done | bytes 1048592 | tf_op jit(solution)/shard_map/reduce_scatter | solution.py:29
  71.6 3.4 collective-permute-start.1
  75.0 2.1 collective-permute-start
  77.1 1.5 collective-permute-start.2
  79.9 1.5 collective-permute-start.6
  81.4 19.7 %collective-permute-done = bf16[64,32,128]{2,0,1:T(8,128)(2,1)S(1)} collective-permute-done((bf16[64,32,128]{2,0,1:T(8,128)(2,1)S(1)}, bf16[64,32,128]{2,0,1:T(8,128)(2,1)S(1)}, u32[]{:S(2)}, u32[]{:S(2)}) %collective-permute-start) | collective-permute-done | bytes 524320 | tf_op jit(solution)/shard_map/ppermute | solution.py:13
  101.1 16.5 %collective-permute-start.5 = (bf16[64,32,128]{2,0,1:T(8,128)(2,1)S(1)}, bf16[64,32,128]{2,0,1:T(8,128)(2,1)S(1)}, u32[]{:S(2)}, u32[]{:S(2)}) collective-permute-start(bf16[64,32,128]{2,0,1:T(8,128)(2,1)S(1)} %copy_bitcast_fusion.2), channel_id=1, source_target_pairs={{8,0},{12,4},{16,8},{20,12},{24,16},{28,20},{32,24},{36,28},{40,32... | collective-permute-start | bytes 1572872 | tf_op jit(solution)/shard_map/ppermute | solution.py:13
  118.4 5.3 collective-permute-start.4
  124.6 3.6 collective-permute-start.7
  129.0 10.7 %collective-permute-done.3 = bf16[64,32,128]{2,0,1:T(8,128)(2,1)S(1)} collective-permute-done((bf16[64,32,128]{2,0,1:T(8,128)(2,1)S(1)}, bf16[64,32,128]{2,0,1:T(8,128)(2,1)S(1)}, u32[]{:S(2)}, u32[]{:S(2)}) %collective-permute-start.3) | collective-permute-done | bytes 524320 | tf_op jit(solution)/shard_map/ppermute | solution.py:13
  141.4 18.4 %collective-permute-done.4 = bf16[64,32,128]{2,0,1:T(8,128)(2,1)S(1)} collective-permute-done((bf16[64,32,128]{2,0,1:T(8,128)(2,1)S(1)}, bf16[64,32,128]{2,0,1:T(8,128)(2,1)S(1)}, u32[]{:S(2)}, u32[]{:S(2)}) %collective-permute-start.4) | collective-permute-done | bytes 524320 | tf_op jit(solution)/shard_map/ppermute | solution.py:13
  163.2 5.9 gather_fusion
  169.1 15.2 %fusion.16 = f32[64,288,128]{2,0,1:T(8,128)} fusion(bf16[288,128,128]{2,1,0:T(8,128)(2,1)} %param.14, bf16[288,64,128]{2,1,0:T(8,128)(2,1)} %gather_fusion, pred[288]{0:T(512)(128)(4,1)S(1)} %get-tuple-element.3), kind=kOutput, calls=%fused_computation.17 | convolution fusion | flops 606339072 | bytes 23593248 | tf_op jit(solution)/shard_map/hsk,srk->hsr/dot_general | solution.py:44
  184.3 15.2 %fusion.2 = f32[32,64,128]{2,0,1:T(8,128)S(1)} fusion(f32[64,288,128]{2,0,1:T(8,128)} %fusion.16, f32[288]{0:T(512)S(1)} %fusion.52, s32[288]{0:T(512)S(1)} %copy-done.4), kind=kOutput, calls=%fused_computation.4 | convolution fusion | flops 905988096 | bytes 10488064 | tf_op jit(solution)/shard_map/hsr,st->htr/dot_general | solution.py:48
  199.5 1.8 fusion.41
  201.4 13.3 %gather_fusion.1 = bf16[288,64,128]{2,1,0:T(8,128)(2,1)} fusion(bf16[64,32,128]{2,0,1:T(8,128)(2,1)S(1)} %bitcast.81, s32[1024]{0:T(1024)S(1)} %pad_clamp_fusion), kind=kCustom, calls=%fused_computation.1 | custom fusion | bytes 9438336 | tf_op jit(solution)/shard_map/jit(_take)/gather | solution.py:52
  214.7 7.0 fusion.19
  221.7 20.5 %fusion.13 = f32[64,288,128]{2,1,0:T(8,128)S(1)} fusion(f32[64,288,128]{2,0,1:T(8,128)S(1)} %fusion.19, f32[288]{0:T(512)S(1)} %fusion.52, s32[288]{0:T(512)S(1)} %get-tuple-element.4), kind=kOutput, calls=%fused_computation.16 | convolution fusion | flops 8153892864 | bytes 18876672 | tf_op jit(solution)/shard_map/hsk,sd->hdk/dot_general | solution.py:57
  242.3 1.6 fusion.57
  244.0 4.4 collective-permute-start.15
  248.4 11.7 %collective-permute-start.13 = (f32[64,32,128]{2,1,0:T(8,128)S(1)}, f32[64,32,128]{2,1,0:T(8,128)S(1)}, u32[]{:S(2)}, u32[]{:S(2)}) collective-permute-start(f32[64,32,128]{2,1,0:T(8,128)S(1)} %get-tuple-element.8), channel_id=1, source_target_pairs={{248,0},{252,4},{0,8},{4,12},{8,16},{12,20},{16,24},{20,28},{24,32... | collective-permute-start | bytes 3145736 | tf_op jit(solution)/shard_map/ppermute | solution.py:13
  260.1 27.4 %collective-permute-done.8 = f32[64,32,128]{2,1,0:T(8,128)S(1)} collective-permute-done((f32[64,32,128]{2,1,0:T(8,128)S(1)}, f32[64,32,128]{2,1,0:T(8,128)S(1)}, u32[]{:S(2)}, u32[]{:S(2)}) %collective-permute-start.8) | collective-permute-done | bytes 1048608 | tf_op jit(solution)/shard_map/ppermute | solution.py:13
  287.5 11.3 %collective-permute-start.11 = (f32[64,32,128]{2,1,0:T(8,128)S(1)}, f32[64,32,128]{2,1,0:T(8,128)S(1)}, u32[]{:S(2)}, u32[]{:S(2)}) collective-permute-start(f32[64,32,128]{2,1,0:T(8,128)S(1)} %get-tuple-element.10), channel_id=1, source_target_pairs={{4,0},{8,4},{12,8},{16,12},{20,16},{24,20},{28,24},{32,28},{36,32}... | collective-permute-start | bytes 3145736 | tf_op jit(solution)/shard_map/ppermute | solution.py:13
  298.8 71.9 %collective-permute-start.10 = (f32[64,32,128]{2,1,0:T(8,128)S(1)}, f32[64,32,128]{2,1,0:T(8,128)S(1)}, u32[]{:S(2)}, u32[]{:S(2)}) collective-permute-start(f32[64,32,128]{2,1,0:T(8,128)S(1)} %get-tuple-element.11), channel_id=1, source_target_pairs={{8,0},{12,4},{16,8},{20,12},{24,16},{28,20},{32,24},{36,28},{40,32... | collective-permute-start | bytes 3145736 | tf_op jit(solution)/shard_map/ppermute | solution.py:13
  370.8 65.4 %collective-permute-done.11 = f32[64,32,128]{2,1,0:T(8,128)S(1)} collective-permute-done((f32[64,32,128]{2,1,0:T(8,128)S(1)}, f32[64,32,128]{2,1,0:T(8,128)S(1)}, u32[]{:S(2)}, u32[]{:S(2)}) %collective-permute-start.11) | collective-permute-done | bytes 1048608 | tf_op jit(solution)/shard_map/ppermute | solution.py:13
  436.2 7.8 collective-permute-done.10
  446.2 69.3 %all-gather.2.cloned.1.call-done = bf16[256,4096]{1,0:T(8,128)(2,1)} async-done(((bf16[64,4096]{1,0:T(8,128)(2,1)}), bf16[256,4096]{1,0:T(8,128)(2,1)}) %all-gather.2.cloned.1.call-update) | async-done | bytes 2097168 | tf_op jit(solution)/shard_map/all_gather | solution.py:67
  515.5 3.0 fusion.24
  518.5 2.9 fusion.12
  521.4 526.6 %all-reduce.2.cloned.1.call-done = f32[64,256]{1,0:T(8,128)} async-done(((f32[64,256]{1,0:T(8,128)}), f32[64,256]{1,0:T(8,128)}) %all-reduce.2.cloned.1.call-update) | async-done | bytes 65552 | tf_op jit(solution)/shard_map/psum | solution.py:76
  1048.0 1.5 copy.63
  (55 shorter events, 13.4 us)
Async XLA Ops:
  7.2 1.0 copy-start
  7.2 4.6 copy-start.4
  7.2 4.6 copy-start.6
  7.2 4.6 copy-start.5
  7.2 63.0 %reduce-scatter.2.cloned.1.call-start = ((), (), s32[]{:S(2)}) async-start(), calls=%async_computation.1 | async-start | bytes 5242880 | tf_op jit(solution)/shard_map/reduce_scatter | solution.py:29
  11.7 503.8 %all-gather.2.cloned.1.call-start = ((), (), s32[]{:S(2)}) async-start(), calls=%async_computation.2 | async-start | bytes 2621440 | tf_op jit(solution)/shard_map/all_gather | solution.py:67
  70.2 70.3 %copy-start.1 = (f32[64,4096]{1,0:T(8,128)S(1)}, f32[64,4096]{1,0:T(8,128)}, u32[]{:S(2)}) copy-start(f32[64,4096]{1,0:T(8,128)} %reduce-scatter.2.cloned.1.call-done) | copy-start | bytes 3145732
  71.6 46.8 %collective-permute-start.1 = (bf16[64,32,128]{2,0,1:T(8,128)(2,1)S(1)}, bf16[64,32,128]{2,0,1:T(8,128)(2,1)S(1)}, u32[]{:S(2)}, u32[]{:S(2)}) collective-permute-start(bf16[64,32,128]{2,0,1:T(8,128)(2,1)S(1)} %copy_bitcast_fusion.2), channel_id=1, source_target_pairs={{244,0},{248,4},{252,8},{0,12},{4,16},{8,20},{12,24},{16,28},{20,3... | collective-permute-start | bytes 1572872 | tf_op jit(solution)/shard_map/ppermute | solution.py:13
  75.0 26.1 %collective-permute-start = (bf16[64,32,128]{2,0,1:T(8,128)(2,1)S(1)}, bf16[64,32,128]{2,0,1:T(8,128)(2,1)S(1)}, u32[]{:S(2)}, u32[]{:S(2)}) collective-permute-start(bf16[64,32,128]{2,0,1:T(8,128)(2,1)S(1)} %copy_bitcast_fusion.2), channel_id=1, source_target_pairs={{240,0},{244,4},{248,8},{252,12},{0,16},{4,20},{8,24},{12,28},{16,... | collective-permute-start | bytes 1572872 | tf_op jit(solution)/shard_map/ppermute | solution.py:13
  77.1 47.5 %collective-permute-start.2 = (bf16[64,32,128]{2,0,1:T(8,128)(2,1)S(1)}, bf16[64,32,128]{2,0,1:T(8,128)(2,1)S(1)}, u32[]{:S(2)}, u32[]{:S(2)}) collective-permute-start(bf16[64,32,128]{2,0,1:T(8,128)(2,1)S(1)} %copy_bitcast_fusion.2), channel_id=1, source_target_pairs={{248,0},{252,4},{0,8},{4,12},{8,16},{12,20},{16,24},{20,28},{24,32... | collective-permute-start | bytes 1572872 | tf_op jit(solution)/shard_map/ppermute | solution.py:13
  79.2 60.4 %collective-permute-start.3 = (bf16[64,32,128]{2,0,1:T(8,128)(2,1)S(1)}, bf16[64,32,128]{2,0,1:T(8,128)(2,1)S(1)}, u32[]{:S(2)}, u32[]{:S(2)}) collective-permute-start(bf16[64,32,128]{2,0,1:T(8,128)(2,1)S(1)} %copy_bitcast_fusion.2), channel_id=1, source_target_pairs={{252,0},{0,4},{4,8},{8,12},{12,16},{16,20},{20,24},{24,28},{28,32}... | collective-permute-start | bytes 1572872 | tf_op jit(solution)/shard_map/ppermute | solution.py:13
  79.9 81.6 %collective-permute-start.6 = (bf16[64,32,128]{2,0,1:T(8,128)(2,1)S(1)}, bf16[64,32,128]{2,0,1:T(8,128)(2,1)S(1)}, u32[]{:S(2)}, u32[]{:S(2)}) collective-permute-start(bf16[64,32,128]{2,0,1:T(8,128)(2,1)S(1)} %copy_bitcast_fusion.2), channel_id=1, source_target_pairs={{12,0},{16,4},{20,8},{24,12},{28,16},{32,20},{36,24},{40,28},{44,3... | collective-permute-start | bytes 1572872 | tf_op jit(solution)/shard_map/ppermute | solution.py:13
  101.1 59.6 %collective-permute-start.5 = (bf16[64,32,128]{2,0,1:T(8,128)(2,1)S(1)}, bf16[64,32,128]{2,0,1:T(8,128)(2,1)S(1)}, u32[]{:S(2)}, u32[]{:S(2)}) collective-permute-start(bf16[64,32,128]{2,0,1:T(8,128)(2,1)S(1)} %copy_bitcast_fusion.2), channel_id=1, source_target_pairs={{8,0},{12,4},{16,8},{20,12},{24,16},{28,20},{32,24},{36,28},{40,32... | collective-permute-start | bytes 1572872 | tf_op jit(solution)/shard_map/ppermute | solution.py:13
  118.4 41.4 %collective-permute-start.4 = (bf16[64,32,128]{2,0,1:T(8,128)(2,1)S(1)}, bf16[64,32,128]{2,0,1:T(8,128)(2,1)S(1)}, u32[]{:S(2)}, u32[]{:S(2)}) collective-permute-start(bf16[64,32,128]{2,0,1:T(8,128)(2,1)S(1)} %copy_bitcast_fusion.2), channel_id=1, source_target_pairs={{4,0},{8,4},{12,8},{16,12},{20,16},{24,20},{28,24},{32,28},{36,32}... | collective-permute-start | bytes 1572872 | tf_op jit(solution)/shard_map/ppermute | solution.py:13
  124.6 37.8 %collective-permute-start.7 = (bf16[64,32,128]{2,0,1:T(8,128)(2,1)S(1)}, bf16[64,32,128]{2,0,1:T(8,128)(2,1)S(1)}, u32[]{:S(2)}, u32[]{:S(2)}) collective-permute-start(bf16[64,32,128]{2,0,1:T(8,128)(2,1)S(1)} %copy_bitcast_fusion.2), channel_id=1, source_target_pairs={{16,0},{20,4},{24,8},{28,12},{32,16},{36,20},{40,24},{44,28},{48,3... | collective-permute-start | bytes 1572872 | tf_op jit(solution)/shard_map/ppermute | solution.py:13
  184.3 15.2 %copy-start.2 = (bf16[64,4096]{1,0:T(8,128)(2,1)S(1)}, bf16[64,4096]{1,0:T(8,128)(2,1)}, u32[]{:S(2)}) copy-start(bf16[64,4096]{1,0:T(8,128)(2,1)} %param.10) | copy-start | bytes 1572868
  243.9 43.6 %collective-permute-start.8 = (f32[64,32,128]{2,1,0:T(8,128)S(1)}, f32[64,32,128]{2,1,0:T(8,128)S(1)}, u32[]{:S(2)}, u32[]{:S(2)}) collective-permute-start(f32[64,32,128]{2,1,0:T(8,128)S(1)} %get-tuple-element.5), channel_id=1, source_target_pairs={{16,0},{20,4},{24,8},{28,12},{32,16},{36,20},{40,24},{44,28},{48,3... | collective-permute-start | bytes 3145736 | tf_op jit(solution)/shard_map/ppermute | solution.py:13
  244.0 54.9 %collective-permute-start.15 = (f32[64,32,128]{2,1,0:T(8,128)S(1)}, f32[64,32,128]{2,1,0:T(8,128)S(1)}, u32[]{:S(2)}, u32[]{:S(2)}) collective-permute-start(f32[64,32,128]{2,1,0:T(8,128)S(1)} %get-tuple-element.6), channel_id=1, source_target_pairs={{240,0},{244,4},{248,8},{252,12},{0,16},{4,20},{8,24},{12,28},{16,... | collective-permute-start | bytes 3145736 | tf_op jit(solution)/shard_map/ppermute | solution.py:13
  248.4 122.4 %collective-permute-start.14 = (f32[64,32,128]{2,1,0:T(8,128)S(1)}, f32[64,32,128]{2,1,0:T(8,128)S(1)}, u32[]{:S(2)}, u32[]{:S(2)}) collective-permute-start(f32[64,32,128]{2,1,0:T(8,128)S(1)} %get-tuple-element.7), channel_id=1, source_target_pairs={{244,0},{248,4},{252,8},{0,12},{4,16},{8,20},{12,24},{16,28},{20,3... | collective-permute-start | bytes 3145736 | tf_op jit(solution)/shard_map/ppermute | solution.py:13
  248.4 122.4 %collective-permute-start.13 = (f32[64,32,128]{2,1,0:T(8,128)S(1)}, f32[64,32,128]{2,1,0:T(8,128)S(1)}, u32[]{:S(2)}, u32[]{:S(2)}) collective-permute-start(f32[64,32,128]{2,1,0:T(8,128)S(1)} %get-tuple-element.8), channel_id=1, source_target_pairs={{248,0},{252,4},{0,8},{4,12},{8,16},{12,20},{16,24},{20,28},{24,32... | collective-permute-start | bytes 3145736 | tf_op jit(solution)/shard_map/ppermute | solution.py:13
  260.1 110.7 %collective-permute-start.12 = (f32[64,32,128]{2,1,0:T(8,128)S(1)}, f32[64,32,128]{2,1,0:T(8,128)S(1)}, u32[]{:S(2)}, u32[]{:S(2)}) collective-permute-start(f32[64,32,128]{2,1,0:T(8,128)S(1)} %get-tuple-element.9), channel_id=1, source_target_pairs={{252,0},{0,4},{4,8},{8,12},{12,16},{16,20},{20,24},{24,28},{28,32}... | collective-permute-start | bytes 3145736 | tf_op jit(solution)/shard_map/ppermute | solution.py:13
  287.5 148.7 %collective-permute-start.11 = (f32[64,32,128]{2,1,0:T(8,128)S(1)}, f32[64,32,128]{2,1,0:T(8,128)S(1)}, u32[]{:S(2)}, u32[]{:S(2)}) collective-permute-start(f32[64,32,128]{2,1,0:T(8,128)S(1)} %get-tuple-element.10), channel_id=1, source_target_pairs={{4,0},{8,4},{12,8},{16,12},{20,16},{24,20},{28,24},{32,28},{36,32}... | collective-permute-start | bytes 3145736 | tf_op jit(solution)/shard_map/ppermute | solution.py:13
  298.8 145.2 %collective-permute-start.10 = (f32[64,32,128]{2,1,0:T(8,128)S(1)}, f32[64,32,128]{2,1,0:T(8,128)S(1)}, u32[]{:S(2)}, u32[]{:S(2)}) collective-permute-start(f32[64,32,128]{2,1,0:T(8,128)S(1)} %get-tuple-element.11), channel_id=1, source_target_pairs={{8,0},{12,4},{16,8},{20,12},{24,16},{28,20},{32,24},{36,28},{40,32... | collective-permute-start | bytes 3145736 | tf_op jit(solution)/shard_map/ppermute | solution.py:13
  370.8 147.8 %copy-start.3 = (bf16[64,256]{1,0:T(8,128)(2,1)S(1)}, bf16[64,256]{1,0:T(8,128)(2,1)}, u32[]{:S(2)}) copy-start(bf16[64,256]{1,0:T(8,128)(2,1)} %param.9) | copy-start | bytes 98308
  370.8 73.2 %collective-permute-start.9 = (f32[64,32,128]{2,1,0:T(8,128)S(1)}, f32[64,32,128]{2,1,0:T(8,128)S(1)}, u32[]{:S(2)}, u32[]{:S(2)}) collective-permute-start(f32[64,32,128]{2,1,0:T(8,128)S(1)} %get-tuple-element.12), channel_id=1, source_target_pairs={{12,0},{16,4},{20,8},{24,12},{28,16},{32,20},{36,24},{40,28},{44,3... | collective-permute-start | bytes 3145736 | tf_op jit(solution)/shard_map/ppermute | solution.py:13
  446.2 601.8 %all-reduce.2.cloned.1.call-start = ((), (), s32[]{:S(2)}) async-start(), calls=%async_computation.3 | async-start | bytes 131072 | tf_op jit(solution)/shard_map/psum | solution.py:76
Sparse Core Ops, SparseCore 0:
  11.8 58.3 reduce-scatter.1
  446.3 69.1 all-gather.1
  518.9 529.0 all-reduce.1
where the time goes:
time: 1060 us
  waiting for transfers between devices  804 us (76%)
  starting transfers between devices  134 us (13%)
  matrix products  67.2 us (6%)
  local copies, waits for them, and re-layouts  31.1 us (3%)
  between operations  14.8 us (1%)
    psum x1, waiting for transfers between devices, per_device(): weight_grad = lax.psum(weight_grad * factor, 'blk')  527 us
    ppermute x16, waiting for transfers between devices, shifted(): return lax.ppermute(block, axis, route)  149 us
    ppermute x16, starting transfers between devices, shifted(): return lax.ppermute(block, axis, route)  134 us
    all_gather x1, waiting for transfers between devices, per_device(): piece = lax.all_gather(grad_proj, 'feat', axis=0, tiled=True)  69.3 us
    reduce_scatter x1, waiting for transfers between devices, per_device(): lax.psum_scatter(lax.dot_general(w_cols, x_t, (((0,), (0,)), ((), ())), p...  58.4 us
  transfers between devices with their start and end apart: 19, of which 9 were waited for; matrix products, arithmetic and copies ran while one was open for 1% of the time, Pallas kernels for 0%

commit v1 on v0

--- a/solution.py
+++ b/solution.py
@@ -73,7 +73,9 @@
     input_grad = jnp.dot(w_cols, piece, preferred_element_type=jnp.float32)
     weight_grad, input_grad = (weight_grad, input_grad)
     factor = 1.0 / math.sqrt(nodes * lax.axis_size("blk"))
-    weight_grad = lax.psum(weight_grad * factor, "blk")
+    part = weight_grad * factor
+    blocks = lax.all_gather(part, "blk", axis=0, tiled=False)
+    weight_grad = blocks.sum(axis=0)
     return (out_t, input_grad.astype(jnp.bfloat16), weight_grad)
 
 

time: 1060 us -> 839 us (0.79)
  the two profiles are of different devices: /device:TPU:26 before, /device:TPU:4 now
where the time goes in v1:
time: 839 us; the launch traced here: 834 us
  waiting for transfers between devices  672 us (80%)
  matrix products  67.2 us (8%)
  starting transfers between devices  41.1 us (5%)
  local copies, waits for them, and re-layouts  29.6 us (4%)
  between operations  14.9 us (2%)
  other arithmetic  8.39 us (1%)
    all_gather x1, waiting for transfers between devices, per_device(): blocks = lax.all_gather(part, 'blk', axis=0, tiled=False)  304 us
    ppermute x16, waiting for transfers between devices, shifted(): return lax.ppermute(block, axis, route)  286 us
    reduce_scatter x1, waiting for transfers between devices, per_device(): lax.psum_scatter(lax.dot_general(w_cols, x_t, (((0,), (0,)), ((), ())), p...  56.9 us
    ppermute x16, starting transfers between devices, shifted(): return lax.ppermute(block, axis, route)  41 us
    all_gather x1, waiting for transfers between devices, per_device(): piece = lax.all_gather(grad_proj, 'feat', axis=0, tiled=True)  25.8 us
    dot_general x1, matrix products, per_device(): jnp.einsum('hsk,sd->hdk', contrib, dest_hot, precision=lax.Precision.HIGH...  20.5 us
  transfers between devices with their start and end apart: 19, of which 12 were waited for; matrix products, arithmetic and copies ran while one was open for 1% of the time, Pallas kernels for 0%

profile of v1, /device:TPU:4, one launch (start us, length us, event | category | flops | bytes accessed | tf_op | source)
XLA Modules:
  0.0 833.6 jit_solution(6405699857895598452)
XLA Ops:
  8.2 3.4 fusion.58
  11.8 56.9 %reduce-scatter.2.cloned.1.call-done = f32[64,4096]{1,0:T(8,128)} async-done(((f32[256,4096]{1,0:T(8,128)}), f32[64,4096]{1,0:T(8,128)}) %reduce-scatter.2.cloned.1.call-update) | async-done | bytes 1048592 | tf_op jit(solution)/shard_map/reduce_scatter | solution.py:29
  68.7 1.4 copy_bitcast_fusion.2
  70.1 3.3 collective-permute-start.1
  73.4 2.7 collective-permute-start
  78.6 6.0 collective-permute-start.6
  84.7 26.6 %collective-permute-done = bf16[64,32,128]{2,0,1:T(8,128)(2,1)S(1)} collective-permute-done((bf16[64,32,128]{2,0,1:T(8,128)(2,1)S(1)}, bf16[64,32,128]{2,0,1:T(8,128)(2,1)S(1)}, u32[]{:S(2)}, u32[]{:S(2)}) %collective-permute-start) | collective-permute-done | bytes 524320 | tf_op jit(solution)/shard_map/ppermute | solution.py:13
  111.3 14.4 %collective-permute-start.5 = (bf16[64,32,128]{2,0,1:T(8,128)(2,1)S(1)}, bf16[64,32,128]{2,0,1:T(8,128)(2,1)S(1)}, u32[]{:S(2)}, u32[]{:S(2)}) collective-permute-start(bf16[64,32,128]{2,0,1:T(8,128)(2,1)S(1)} %copy_bitcast_fusion.2), channel_id=1, source_target_pairs={{8,0},{12,4},{16,8},{20,12},{24,16},{28,20},{32,24},{36,28},{40,32... | collective-permute-start | bytes 1572872 | tf_op jit(solution)/shard_map/ppermute | solution.py:13
  128.3 6.6 collective-permute-done.3
  136.7 19.0 %collective-permute-done.4 = bf16[64,32,128]{2,0,1:T(8,128)(2,1)S(1)} collective-permute-done((bf16[64,32,128]{2,0,1:T(8,128)(2,1)S(1)}, bf16[64,32,128]{2,0,1:T(8,128)(2,1)S(1)}, u32[]{:S(2)}, u32[]{:S(2)}) %collective-permute-start.4) | collective-permute-done | bytes 524320 | tf_op jit(solution)/shard_map/ppermute | solution.py:13
  158.2 7.8 collective-permute-done.7
  166.9 5.9 gather_fusion
  172.7 15.2 %fusion.16 = f32[64,288,128]{2,0,1:T(8,128)} fusion(bf16[288,128,128]{2,1,0:T(8,128)(2,1)} %param.14, bf16[288,64,128]{2,1,0:T(8,128)(2,1)} %gather_fusion, pred[288]{0:T(512)(128)(4,1)S(1)} %get-tuple-element.3), kind=kOutput, calls=%fused_computation.17 | convolution fusion | flops 606339072 | bytes 23593248 | tf_op jit(solution)/shard_map/hsk,srk->hsr/dot_general | solution.py:44
  187.9 15.2 %fusion.2 = f32[32,64,128]{2,0,1:T(8,128)S(1)} fusion(f32[64,288,128]{2,0,1:T(8,128)} %fusion.16, f32[288]{0:T(512)S(1)} %fusion.52, s32[288]{0:T(512)S(1)} %copy-done.4), kind=kOutput, calls=%fused_computation.4 | convolution fusion | flops 905988096 | bytes 10488064 | tf_op jit(solution)/shard_map/hsr,st->htr/dot_general | solution.py:48
  203.2 1.8 fusion.41
  205.1 13.3 %gather_fusion.1 = bf16[288,64,128]{2,1,0:T(8,128)(2,1)} fusion(bf16[64,32,128]{2,0,1:T(8,128)(2,1)S(1)} %bitcast.82, s32[1024]{0:T(1024)S(1)} %pad_clamp_fusion), kind=kCustom, calls=%fused_computation.1 | custom fusion | bytes 9438336 | tf_op jit(solution)/shard_map/jit(_take)/gather | solution.py:52
  218.4 7.0 fusion.19
  225.4 20.5 %fusion.13 = f32[64,288,128]{2,1,0:T(8,128)S(1)} fusion(f32[64,288,128]{2,0,1:T(8,128)S(1)} %fusion.19, f32[288]{0:T(512)S(1)} %fusion.52, s32[288]{0:T(512)S(1)} %get-tuple-element.4), kind=kOutput, calls=%fused_computation.16 | convolution fusion | flops 8153892864 | bytes 18876672 | tf_op jit(solution)/shard_map/hsk,sd->hdk/dot_general | solution.py:57
  246.0 1.6 fusion.57
  247.5 6.2 collective-permute-start.8
  253.9 5.8 collective-permute-start.12
  259.7 112.2 %collective-permute-done.8 = f32[64,32,128]{2,1,0:T(8,128)S(1)} collective-permute-done((f32[64,32,128]{2,1,0:T(8,128)S(1)}, f32[64,32,128]{2,1,0:T(8,128)S(1)}, u32[]{:S(2)}, u32[]{:S(2)}) %collective-permute-start.8) | collective-permute-done | bytes 1048608 | tf_op jit(solution)/shard_map/ppermute | solution.py:13
  372.3 6.2 collective-permute-done.13
  378.6 54.1 %collective-permute-done.11 = f32[64,32,128]{2,1,0:T(8,128)S(1)} collective-permute-done((f32[64,32,128]{2,1,0:T(8,128)S(1)}, f32[64,32,128]{2,1,0:T(8,128)S(1)}, u32[]{:S(2)}, u32[]{:S(2)}) %collective-permute-start.11) | collective-permute-done | bytes 1048608 | tf_op jit(solution)/shard_map/ppermute | solution.py:13
  432.7 34.5 %collective-permute-done.10 = f32[64,32,128]{2,1,0:T(8,128)S(1)} collective-permute-done((f32[64,32,128]{2,1,0:T(8,128)S(1)}, f32[64,32,128]{2,1,0:T(8,128)S(1)}, u32[]{:S(2)}, u32[]{:S(2)}) %collective-permute-start.10) | collective-permute-done | bytes 1048608 | tf_op jit(solution)/shard_map/ppermute | solution.py:13
  467.2 18.8 %collective-permute-done.9 = f32[64,32,128]{2,1,0:T(8,128)S(1)} collective-permute-done((f32[64,32,128]{2,1,0:T(8,128)S(1)}, f32[64,32,128]{2,1,0:T(8,128)S(1)}, u32[]{:S(2)}, u32[]{:S(2)}) %collective-permute-start.9) | collective-permute-done | bytes 1048608 | tf_op jit(solution)/shard_map/ppermute | solution.py:13
  486.0 1.2 fusion.40
  488.2 25.8 %all-gather.4.cloned.1.call-done = bf16[256,4096]{1,0:T(8,128)(2,1)} async-done(((bf16[64,4096]{1,0:T(8,128)(2,1)}), bf16[256,4096]{1,0:T(8,128)(2,1)}) %all-gather.4.cloned.1.call-update) | async-done | bytes 2097168 | tf_op jit(solution)/shard_map/all_gather | solution.py:67
  514.0 3.0 fusion.24
  517.0 2.9 fusion.12
  519.9 303.8 %all-gather.6.cloned.1.call-done = f32[4096,256]{1,0:T(8,128)} async-done(((f32[64,256]{1,0:T(8,128)}), f32[4096,256]{1,0:T(8,128)}) %all-gather.6.cloned.1.call-update) | async-done | bytes 4194320 | tf_op jit(solution)/shard_map/all_gather | solution.py:77
  823.7 3.1 reduce_sum.9
  (55 shorter events, 12.5 us)
Async XLA Ops:
  7.2 1.0 copy-start
  7.2 4.6 copy-start.4
  7.2 4.6 copy-start.6
  7.2 4.6 copy-start.5
  7.2 61.5 %reduce-scatter.2.cloned.1.call-start = ((), (), s32[]{:S(2)}) async-start(), calls=%async_computation.1 | async-start | bytes 5242880 | tf_op jit(solution)/shard_map/reduce_scatter | solution.py:29
  11.7 502.3 %all-gather.4.cloned.1.call-start = ((), (), s32[]{:S(2)}) async-start(), calls=%async_computation.2 | async-start | bytes 2621440 | tf_op jit(solution)/shard_map/all_gather | solution.py:67
  68.7 67.1 %copy-start.1 = (f32[64,4096]{1,0:T(8,128)S(1)}, f32[64,4096]{1,0:T(8,128)}, u32[]{:S(2)}) copy-start(f32[64,4096]{1,0:T(8,128)} %reduce-scatter.2.cloned.1.call-done) | copy-start | bytes 3145732
  70.1 56.4 %collective-permute-start.1 = (bf16[64,32,128]{2,0,1:T(8,128)(2,1)S(1)}, bf16[64,32,128]{2,0,1:T(8,128)(2,1)S(1)}, u32[]{:S(2)}, u32[]{:S(2)}) collective-permute-start(bf16[64,32,128]{2,0,1:T(8,128)(2,1)S(1)} %copy_bitcast_fusion.2), channel_id=1, source_target_pairs={{244,0},{248,4},{252,8},{0,12},{4,16},{8,20},{12,24},{16,28},{20,3... | collective-permute-start | bytes 1572872 | tf_op jit(solution)/shard_map/ppermute | solution.py:13
  73.4 37.8 %collective-permute-start = (bf16[64,32,128]{2,0,1:T(8,128)(2,1)S(1)}, bf16[64,32,128]{2,0,1:T(8,128)(2,1)S(1)}, u32[]{:S(2)}, u32[]{:S(2)}) collective-permute-start(bf16[64,32,128]{2,0,1:T(8,128)(2,1)S(1)} %copy_bitcast_fusion.2), channel_id=1, source_target_pairs={{240,0},{244,4},{248,8},{252,12},{0,16},{4,20},{8,24},{12,28},{16,... | collective-permute-start | bytes 1572872 | tf_op jit(solution)/shard_map/ppermute | solution.py:13
  76.1 51.2 %collective-permute-start.2 = (bf16[64,32,128]{2,0,1:T(8,128)(2,1)S(1)}, bf16[64,32,128]{2,0,1:T(8,128)(2,1)S(1)}, u32[]{:S(2)}, u32[]{:S(2)}) collective-permute-start(bf16[64,32,128]{2,0,1:T(8,128)(2,1)S(1)} %copy_bitcast_fusion.2), channel_id=1, source_target_pairs={{248,0},{252,4},{0,8},{4,12},{8,16},{12,20},{16,24},{20,28},{24,32... | collective-permute-start | bytes 1572872 | tf_op jit(solution)/shard_map/ppermute | solution.py:13
  77.7 57.2 %collective-permute-start.3 = (bf16[64,32,128]{2,0,1:T(8,128)(2,1)S(1)}, bf16[64,32,128]{2,0,1:T(8,128)(2,1)S(1)}, u32[]{:S(2)}, u32[]{:S(2)}) collective-permute-start(bf16[64,32,128]{2,0,1:T(8,128)(2,1)S(1)} %copy_bitcast_fusion.2), channel_id=1, source_target_pairs={{252,0},{0,4},{4,8},{8,12},{12,16},{16,20},{20,24},{24,28},{28,32}... | collective-permute-start | bytes 1572872 | tf_op jit(solution)/shard_map/ppermute | solution.py:13
  78.6 78.8 %collective-permute-start.6 = (bf16[64,32,128]{2,0,1:T(8,128)(2,1)S(1)}, bf16[64,32,128]{2,0,1:T(8,128)(2,1)S(1)}, u32[]{:S(2)}, u32[]{:S(2)}) collective-permute-start(bf16[64,32,128]{2,0,1:T(8,128)(2,1)S(1)} %copy_bitcast_fusion.2), channel_id=1, source_target_pairs={{12,0},{16,4},{20,8},{24,12},{28,16},{32,20},{36,24},{40,28},{44,3... | collective-permute-start | bytes 1572872 | tf_op jit(solution)/shard_map/ppermute | solution.py:13
  111.3 45.3 %collective-permute-start.5 = (bf16[64,32,128]{2,0,1:T(8,128)(2,1)S(1)}, bf16[64,32,128]{2,0,1:T(8,128)(2,1)S(1)}, u32[]{:S(2)}, u32[]{:S(2)}) collective-permute-start(bf16[64,32,128]{2,0,1:T(8,128)(2,1)S(1)} %copy_bitcast_fusion.2), channel_id=1, source_target_pairs={{8,0},{12,4},{16,8},{20,12},{24,16},{28,20},{32,24},{36,28},{40,32... | collective-permute-start | bytes 1572872 | tf_op jit(solution)/shard_map/ppermute | solution.py:13
  126.5 29.2 %collective-permute-start.4 = (bf16[64,32,128]{2,0,1:T(8,128)(2,1)S(1)}, bf16[64,32,128]{2,0,1:T(8,128)(2,1)S(1)}, u32[]{:S(2)}, u32[]{:S(2)}) collective-permute-start(bf16[64,32,128]{2,0,1:T(8,128)(2,1)S(1)} %copy_bitcast_fusion.2), channel_id=1, source_target_pairs={{4,0},{8,4},{12,8},{16,12},{20,16},{24,20},{28,24},{32,28},{36,32}... | collective-permute-start | bytes 1572872 | tf_op jit(solution)/shard_map/ppermute | solution.py:13
  127.3 38.7 %collective-permute-start.7 = (bf16[64,32,128]{2,0,1:T(8,128)(2,1)S(1)}, bf16[64,32,128]{2,0,1:T(8,128)(2,1)S(1)}, u32[]{:S(2)}, u32[]{:S(2)}) collective-permute-start(bf16[64,32,128]{2,0,1:T(8,128)(2,1)S(1)} %copy_bitcast_fusion.2), channel_id=1, source_target_pairs={{16,0},{20,4},{24,8},{28,12},{32,16},{36,20},{40,24},{44,28},{48,3... | collective-permute-start | bytes 1572872 | tf_op jit(solution)/shard_map/ppermute | solution.py:13
  187.9 15.2 %copy-start.2 = (bf16[64,4096]{1,0:T(8,128)(2,1)S(1)}, bf16[64,4096]{1,0:T(8,128)(2,1)}, u32[]{:S(2)}) copy-start(bf16[64,4096]{1,0:T(8,128)(2,1)} %param.10) | copy-start | bytes 1572868
  247.5 124.4 %collective-permute-start.8 = (f32[64,32,128]{2,1,0:T(8,128)S(1)}, f32[64,32,128]{2,1,0:T(8,128)S(1)}, u32[]{:S(2)}, u32[]{:S(2)}) collective-permute-start(f32[64,32,128]{2,1,0:T(8,128)S(1)} %get-tuple-element.5), channel_id=1, source_target_pairs={{16,0},{20,4},{24,8},{28,12},{32,16},{36,20},{40,24},{44,28},{48,3... | collective-permute-start | bytes 3145736 | tf_op jit(solution)/shard_map/ppermute | solution.py:13
  253.7 118.4 %collective-permute-start.15 = (f32[64,32,128]{2,1,0:T(8,128)S(1)}, f32[64,32,128]{2,1,0:T(8,128)S(1)}, u32[]{:S(2)}, u32[]{:S(2)}) collective-permute-start(f32[64,32,128]{2,1,0:T(8,128)S(1)} %get-tuple-element.6), channel_id=1, source_target_pairs={{240,0},{244,4},{248,8},{252,12},{0,16},{4,20},{8,24},{12,28},{16,... | collective-permute-start | bytes 3145736 | tf_op jit(solution)/shard_map/ppermute | solution.py:13
  253.9 118.3 %collective-permute-start.14 = (f32[64,32,128]{2,1,0:T(8,128)S(1)}, f32[64,32,128]{2,1,0:T(8,128)S(1)}, u32[]{:S(2)}, u32[]{:S(2)}) collective-permute-start(f32[64,32,128]{2,1,0:T(8,128)S(1)} %get-tuple-element.7), channel_id=1, source_target_pairs={{244,0},{248,4},{252,8},{0,12},{4,16},{8,20},{12,24},{16,28},{20,3... | collective-permute-start | bytes 3145736 | tf_op jit(solution)/shard_map/ppermute | solution.py:13
  253.9 124.7 %collective-permute-start.13 = (f32[64,32,128]{2,1,0:T(8,128)S(1)}, f32[64,32,128]{2,1,0:T(8,128)S(1)}, u32[]{:S(2)}, u32[]{:S(2)}) collective-permute-start(f32[64,32,128]{2,1,0:T(8,128)S(1)} %get-tuple-element.8), channel_id=1, source_target_pairs={{248,0},{252,4},{0,8},{4,12},{8,16},{12,20},{16,24},{20,28},{24,32... | collective-permute-start | bytes 3145736 | tf_op jit(solution)/shard_map/ppermute | solution.py:13
  253.9 124.7 %collective-permute-start.12 = (f32[64,32,128]{2,1,0:T(8,128)S(1)}, f32[64,32,128]{2,1,0:T(8,128)S(1)}, u32[]{:S(2)}, u32[]{:S(2)}) collective-permute-start(f32[64,32,128]{2,1,0:T(8,128)S(1)} %get-tuple-element.9), channel_id=1, source_target_pairs={{252,0},{0,4},{4,8},{8,12},{12,16},{16,20},{20,24},{24,28},{28,32}... | collective-permute-start | bytes 3145736 | tf_op jit(solution)/shard_map/ppermute | solution.py:13
  371.9 60.8 %collective-permute-start.11 = (f32[64,32,128]{2,1,0:T(8,128)S(1)}, f32[64,32,128]{2,1,0:T(8,128)S(1)}, u32[]{:S(2)}, u32[]{:S(2)}) collective-permute-start(f32[64,32,128]{2,1,0:T(8,128)S(1)} %get-tuple-element.10), channel_id=1, source_target_pairs={{4,0},{8,4},{12,8},{16,12},{20,16},{24,20},{28,24},{32,28},{36,32}... | collective-permute-start | bytes 3145736 | tf_op jit(solution)/shard_map/ppermute | solution.py:13
  372.1 95.0 %collective-permute-start.10 = (f32[64,32,128]{2,1,0:T(8,128)S(1)}, f32[64,32,128]{2,1,0:T(8,128)S(1)}, u32[]{:S(2)}, u32[]{:S(2)}) collective-permute-start(f32[64,32,128]{2,1,0:T(8,128)S(1)} %get-tuple-element.11), channel_id=1, source_target_pairs={{8,0},{12,4},{16,8},{20,12},{24,16},{28,20},{32,24},{36,28},{40,32... | collective-permute-start | bytes 3145736 | tf_op jit(solution)/shard_map/ppermute | solution.py:13
  372.2 144.8 %copy-start.3 = (bf16[64,256]{1,0:T(8,128)(2,1)S(1)}, bf16[64,256]{1,0:T(8,128)(2,1)}, u32[]{:S(2)}) copy-start(bf16[64,256]{1,0:T(8,128)(2,1)} %param.9) | copy-start | bytes 98308
  372.3 113.7 %collective-permute-start.9 = (f32[64,32,128]{2,1,0:T(8,128)S(1)}, f32[64,32,128]{2,1,0:T(8,128)S(1)}, u32[]{:S(2)}, u32[]{:S(2)}) collective-permute-start(f32[64,32,128]{2,1,0:T(8,128)S(1)} %get-tuple-element.12), channel_id=1, source_target_pairs={{12,0},{16,4},{20,8},{24,12},{28,16},{32,20},{36,24},{40,28},{44,3... | collective-permute-start | bytes 3145736 | tf_op jit(solution)/shard_map/ppermute | solution.py:13
  488.1 335.6 %all-gather.6.cloned.1.call-start = ((), (), s32[]{:S(2)}) async-start(), calls=%async_computation.3 | async-start | bytes 4259840 | tf_op jit(solution)/shard_map/all_gather | solution.py:77
Sparse Core Ops, SparseCore 0:
  11.8 56.8 reduce-scatter.1
  488.3 25.6 all-gather.3
  517.1 306.5 all-gather.5
